TPU v7x, 32 devices: a whole 2x2x4 slice. The times are simulated.
32 devices in a mesh: head: 4 (over z), tok: 8 (over y, x, core).
Axes of the slice: x: 2, y: 2, z: 4, core: 2. Of those that a mesh axis runs over, the one named last changes fastest.
Arguments:
- teacher_q: bfloat16 [1024, 1024], P('tok', 'head'), may hold values from -48 to 48
- student_q: bfloat16 [1024, 1024], P('tok', 'head'), may hold values from -48 to 48
- owner_table: int32 [8, 8], replicated, may hold values from -1 to 7, as said below
Outputs:
- student_grad: bfloat16 [1024, 1024], P('tok', 'head')
- divergence: float32 [16], P('head')
Inputs may be any that keep to these rules, and one draw needn't show every extreme that they name: `owner_table`: Symmetric; every diagonal entry is an owner; an owner is a tok index; each tok index owns at most 2 pairs i <= j, and some tok index owns exactly 2 in every draw.
All inputs are finite; a program needn't handle non-finite values.
Results may differ from a plain program's by a relative error of at most 0.0049.
Values may be sent and summed in bfloat16 or wider, within the bound.
A program may use at most 64 MiB of HBM per device.

v0:
```python
import jax
import jax.numpy as jnp
from jax import lax
from jax.sharding import PartitionSpec as P

HEAD_DIM = 64


floor_value = -1e30
distill_weight = 32.0


def split_heads(block):
    return block.reshape(block.shape[0], -1, HEAD_DIM)


def tile_scores(left_block, right_block):
    return jnp.einsum(
        "ahd,bhd->hab", left_block, right_block, preferred_element_type=jnp.float32
    ) * HEAD_DIM ** (-0.5)


def reduced_totals(scores, reduce_axis):
    highest = jnp.max(scores, axis=reduce_axis)
    return (
        highest,
        jnp.sum(jnp.exp(scores - jnp.expand_dims(highest, reduce_axis)), axis=reduce_axis),
    )


def fold_totals(earlier, later):
    teacher_top = jnp.maximum(earlier[0], later[0])
    student_top = jnp.maximum(earlier[2], later[2])
    teacher_sum = earlier[1] * jnp.exp(earlier[0] - teacher_top) + later[1] * jnp.exp(
        later[0] - teacher_top
    )
    student_sum = earlier[3] * jnp.exp(earlier[2] - student_top) + later[3] * jnp.exp(
        later[2] - student_top
    )
    return (teacher_top, teacher_sum, student_top, student_sum)


def pair_totals(teacher_left, teacher_right, student_left, student_right):
    teacher_scores = tile_scores(teacher_left, teacher_right)
    student_scores = tile_scores(student_left, student_right)
    row_side = reduced_totals(teacher_scores, 2) + reduced_totals(student_scores, 2)
    column_side = reduced_totals(teacher_scores, 1) + reduced_totals(student_scores, 1)
    return (row_side, column_side)


def to_logsum(totals):
    return (totals[0] + jnp.log(totals[1]), totals[2] + jnp.log(totals[3]))


def blank_totals(head_count, block_rows):
    return (
        jnp.full((head_count, block_rows), floor_value, jnp.float32),
        jnp.zeros((head_count, block_rows), jnp.float32),
        jnp.full((head_count, block_rows), floor_value, jnp.float32),
        jnp.zeros((head_count, block_rows), jnp.float32),
    )


def gathered_block(gathered, position, block_rows):
    return split_heads(lax.dynamic_slice_in_dim(gathered, position * block_rows, block_rows, 0))


def pair_gradient(
    teacher_left, teacher_right, student_left, student_right, left_logsum, right_logsum
):
    teacher_scores = tile_scores(teacher_left, teacher_right)
    student_scores = tile_scores(student_left, student_right)
    teacher_rows = jnp.exp(teacher_scores - left_logsum[0][:, :, None])
    student_rows = jnp.exp(student_scores - left_logsum[1][:, :, None])
    teacher_cols = jnp.exp(teacher_scores - right_logsum[0][:, None, :])
    student_cols = jnp.exp(student_scores - right_logsum[1][:, None, :])
    score_gap = teacher_scores - student_scores
    symmetric = (student_rows - teacher_rows + (student_cols - teacher_cols)).astype(jnp.bfloat16)
    left_grad = jnp.einsum(
        "hab,bhd->ahd", symmetric, student_right, preferred_element_type=jnp.float32
    )
    right_grad = jnp.einsum(
        "hab,ahd->bhd", symmetric, student_left, preferred_element_type=jnp.float32
    )
    left_div = jnp.sum(teacher_rows * score_gap, axis=(1, 2))
    right_div = jnp.sum(teacher_cols * score_gap, axis=(1, 2))
    return (left_grad, right_grad, left_div, right_div)


def per_device(teacher_q, student_q, owner_table):
    block_count = lax.axis_size("tok")
    own_index = lax.axis_index("tok")
    block_rows = teacher_q.shape[0]
    row_width = teacher_q.shape[1]
    head_count = row_width // HEAD_DIM
    home_teacher = split_heads(teacher_q)
    home_student = split_heads(student_q)
    every_teacher, every_student = (
        lax.all_gather(teacher_q, "tok", axis=0, tiled=True),
        lax.all_gather(student_q, "tok", axis=0, tiled=True),
    )
    inside_row = owner_table[own_index] >= 0
    column_total = jnp.sum(inside_row.astype(jnp.int32))
    columns = jnp.nonzero(inside_row, size=block_count, fill_value=0)[0].astype(jnp.int32)

    def row_turn(slot_index, totals):
        column = columns[slot_index]
        row_side, unused = pair_totals(
            home_teacher,
            gathered_block(every_teacher, column, block_rows),
            home_student,
            gathered_block(every_student, column, block_rows),
        )
        return fold_totals(totals, row_side)

    own_totals = lax.fori_loop(0, column_total, row_turn, blank_totals(head_count, block_rows))
    own_logsum = to_logsum(own_totals)
    every_tlog, every_slog = (
        lax.all_gather(own_logsum[0], "tok", axis=1, tiled=True),
        lax.all_gather(own_logsum[1], "tok", axis=1, tiled=True),
    )

    def gradient_turn(slot_index, carry):
        gradient, running = carry
        column = columns[slot_index]
        column_logsum = (
            lax.dynamic_slice_in_dim(every_tlog, column * block_rows, block_rows, 1),
            lax.dynamic_slice_in_dim(every_slog, column * block_rows, block_rows, 1),
        )
        pieces = pair_gradient(
            home_teacher,
            gathered_block(every_teacher, column, block_rows),
            home_student,
            gathered_block(every_student, column, block_rows),
            own_logsum,
            column_logsum,
        )
        return (gradient + pieces[0], running + pieces[2])

    start_grad = jnp.zeros((block_rows, head_count, HEAD_DIM), jnp.float32)
    gradient, divergence = lax.fori_loop(
        0, column_total, gradient_turn, (start_grad, jnp.zeros((head_count,), jnp.float32))
    )
    own_grad = gradient.reshape(block_rows, row_width)
    divergence = divergence + jnp.sum(own_logsum[1] - own_logsum[0], axis=1)
    divergence = lax.psum(divergence, "tok") / (block_rows * block_count)
    student_grad = (own_grad * (distill_weight * HEAD_DIM ** (-0.5))).astype(jnp.bfloat16)
    return (student_grad, divergence)


def solution(mesh):
    placed = (P("tok", "head"), P("tok", "head"), P())
    return jax.shard_map(
        per_device,
        mesh=mesh,
        in_specs=placed,
        out_specs=(P("tok", "head"), P("head")),
        check_vma=False,
    )
```

profile of v0, /device:TPU:0, one launch (start us, length us, event | category | flops | bytes accessed | tf_op | source)
XLA Modules:
  0.0 79.0 jit_solution(16219702087354555553)
XLA Ops:
  0.6 1.3 %fusion.12 = s32[]{:T(128)} fusion(s32[8,8]{1,0:T(8,128)} %param.9, s32[]{:T(128)S(6)} %select_n.43), kind=kLoop, calls=%fused_computation.42 | loop fusion | flops 23 | bytes 40 | tf_op jit(solution)/shard_map/reduce_sum | solution.py:103
  2.0 0.7 fusion.11
  2.7 0.2 reduce-window.14
  2.9 0.6 scatter_custom_fusion
  3.5 0.2 reduce-window.15
  3.6 0.7 compare_select_fusion.3
  4.3 0.0 copy-start
  4.3 1.0 %copy.12 = bf16[128,256]{0,1:T(8,128)(2,1)S(1)} copy(bf16[128,256]{1,0:T(8,128)(2,1)} %param.7) | data formatting | bytes 131072 | tf_op args[0]
  5.3 0.0 copy-done
  5.3 0.1 copy.10
  5.4 11.5 %all_gather.12 = bf16[1024,256]{0,1:T(8,128)(2,1)S(1)} all-gather(bf16[128,256]{0,1:T(8,128)(2,1)S(1)} %copy.10), channel_id=1, replica_groups=mesh['head'=4,'tok'=8] {'tok'}, dimensions={0}, use_global_device_ids=true | all-gather | bytes 589824 | tf_op jit(solution)/shard_map/all_gather | solution.py:100
  16.9 9.9 %all_gather.13 = bf16[1024,256]{0,1:T(8,128)(2,1)S(1)} all-gather(bf16[128,256]{0,1:T(8,128)(2,1)S(1)} %copy.12), channel_id=1, replica_groups=mesh['head'=4,'tok'=8] {'tok'}, dimensions={0}, use_global_device_ids=true | all-gather | bytes 589824 | tf_op jit(solution)/shard_map/all_gather | solution.py:99
  26.8 6.2 %while.28 = (s32[]{:T(128)}, f32[4,128]{1,0:T(4,128)S(1)}, f32[4,128]{1,0:T(4,128)S(1)}, f32[4,128]{1,0:T(4,128)S(1)}, f32[4,128]{1,0:T(4,128)S(1)}, /*index=5*/...) while((s32[]{:T(128)}, f32[4,128]{1,0:T(4,128)S(1)}, ...), condition=%wide.region_9.10_spmd, body=%wide.region_4.9_spmd.sunk | while | flops 17305608 | bytes 1609985 | solution.py:116
  27.5 0.7 dynamic_slice.47
  28.9 0.3 fusion.41
  29.2 0.1 exponential_reduce_fusion.5
  29.3 0.3 fusion.40
  29.5 0.1 exponential_reduce_fusion.4
  30.3 0.7 dynamic_slice.47
  31.7 0.3 fusion.41
  32.0 0.1 exponential_reduce_fusion.5
  32.0 0.3 fusion.40
  32.3 0.1 exponential_reduce_fusion.4
  33.0 0.1 subtract_reduce_fusion
  33.1 11.7 %all_gather.15 = f32[4,1024]{1,0:T(4,128)S(1)} all-gather(f32[4,128]{1,0:T(4,128)S(1)} %get-tuple-element.441), channel_id=1, replica_groups=mesh['head'=4,'tok'=8] {'tok'}, dimensions={1}, use_global_device_ids=true | all-gather | bytes 18432 | tf_op jit(solution)/shard_map/all_gather | solution.py:119
  44.8 9.6 %all_gather.14 = f32[4,1024]{1,0:T(4,128)S(1)} all-gather(f32[4,128]{1,0:T(4,128)S(1)} %get-tuple-element.438), channel_id=1, replica_groups=mesh['head'=4,'tok'=8] {'tok'}, dimensions={1}, use_global_device_ids=true | all-gather | bytes 18432 | tf_op jit(solution)/shard_map/all_gather | solution.py:120
  54.4 6.8 %while.29 = (s32[]{:T(128)}, f32[128,4,64]{0,2,1:T(8,128)S(1)}, f32[4]{0:T(128)S(1)}, s32[]{:T(128)}, s32[8]{0:T(128)S(1)}, /*index=5*/bf16[1024,256]{0,1:T(8,12...) while((s32[]{:T(128)}, f32[128,4,64]{0,2,1:T(8,128)S(1)}, ...), condition=%wide.region_12.13_spmd, body=%wide.region_10.12_spmd.sunk | while | flops 26116104 | bytes 2181457 | solution.py:141
  55.1 0.7 dynamic_slice.50
  56.5 0.2 convolution_multiply_fusion.5
  56.7 0.4 multiply_reduce_fusion.2
  57.1 0.4 fusion.47
  58.1 0.7 dynamic_slice.50
  59.6 0.2 convolution_multiply_fusion.5
  59.8 0.4 multiply_reduce_fusion.2
  60.2 0.4 fusion.47
  61.2 16.5 %psum.7 = f32[4]{0:T(128)S(1)} all-reduce(f32[4]{0:T(128)S(1)} %add.75), channel_id=1, replica_groups=mesh['head'=4,'tok'=8] {'tok'}, use_global_device_ids=true, to_apply=%region_14.15 | all-reduce | flops 4 | bytes 32 | tf_op jit(solution)/shard_map/psum | solution.py:146
  77.8 0.5 broadcast_multiply_fusion
  78.3 0.7 copy.14
  (22 shorter events, 0.3 us)
Async XLA Ops:
  4.3 1.0 %copy-start = (bf16[128,256]{1,0:T(8,128)(2,1)S(1)}, bf16[128,256]{1,0:T(8,128)(2,1)}, u32[]{:S(2)}) copy-start(bf16[128,256]{1,0:T(8,128)(2,1)} %param.8) | copy-start | bytes 196612
where the time goes:
time: 79.5 us; the launch traced here: 79 us
  blocking collectives  59.2 us (74%)
  loops' own time  6.89 us (9%)
  local copies, waits for them, and re-layouts  4.75 us (6%)
  other arithmetic  4.62 us (6%)
  matrix products  2.91 us (4%)
    psum x1, blocking collectives, per_device(): divergence = lax.psum(divergence, 'tok') / (block_rows * block_count)  16.5 us
    all_gather x1, blocking collectives, per_device(): lax.all_gather(own_logsum[0], 'tok', axis=1, tiled=True)  11.7 us
    all_gather x1, blocking collectives, per_device(): lax.all_gather(student_q, 'tok', axis=0, tiled=True)  11.5 us
    all_gather x1, blocking collectives, per_device(): lax.all_gather(teacher_q, 'tok', axis=0, tiled=True)  9.94 us
    all_gather x1, blocking collectives, per_device(): lax.all_gather(own_logsum[1], 'tok', axis=1, tiled=True)  9.56 us
    another operation x1, loops' own time, per_device(): lax.fori_loop(0, column_total, gradient_turn, (start_grad, jnp.zeros((hea...  3.45 us
    another operation x1, loops' own time, per_device(): lax.fori_loop(0, column_total, row_turn, blank_totals(head_count, block_r...  3.44 us
    dot_general x8, matrix products, tile_scores(): jnp.einsum('ahd,bhd->hab', left_block, right_block, preferred_element_typ...  2.19 us

commit v1 on v0

v1 whole, which is shorter than its diff:
```python
import functools
import math

import jax
import jax.numpy as jnp
from jax import lax
from jax.experimental import pallas as pl
from jax.experimental.pallas import tpu as pltpu
from jax.sharding import PartitionSpec as P

HEAD_DIM = 64
LANES = 128
floor_value = -1e30
distill_weight = 32.0
score_factor = HEAD_DIM ** (-0.5) * math.log2(math.e)
MESH = pl.DeviceIdType.MESH


def repeat(count, body, init=None):
    if count <= 8:
        for step in range(count):
            init = body(step, init)
        return init
    return lax.fori_loop(0, count, body, init)


def kernel(
    n, teacher_hbm, student_hbm, table, grad_ref, div_ref,
    teacher, student, own_teacher, own_student, t_scores, s_scores, t_top, s_top,
    t_log, s_log, row_part, stats, total,
    local_sem, send_sem, recv_sem, pass_send, pass_recv, stat_send, stat_recv,
):
    rows, width = teacher_hbm.shape
    pairs = width // LANES
    heads = width // HEAD_DIM
    group = LANES // HEAD_DIM
    chips = n // 2
    side = math.isqrt(chips)
    side = side if side * side == chips else 1
    span = chips // side
    me = lax.axis_index("tok")
    head_at = lax.axis_index("head")
    chip, core = me // 2, me % 2
    sibling = chip * 2 + 1 - core

    def spot(tok):
        return (head_at, tok)

    def shifted(k, sign):
        high = (chip // span + sign * (k // span) + side) % side
        low = (chip % span + sign * (k % span) + span) % span
        return high * span + low

    barrier = pltpu.get_barrier_semaphore()

    def greet(d, carry):
        pl.semaphore_signal(barrier, inc=1, device_id=spot((me + d + 1) % n), device_id_type=MESH)
        return carry

    loads = [
        pltpu.make_async_copy(teacher_hbm, teacher.at[me], local_sem.at[0]),
        pltpu.make_async_copy(student_hbm, student.at[me], local_sem.at[1]),
    ]
    for load in loads:
        load.start()
    repeat(n - 1, greet)
    sources = ((teacher_hbm, teacher), (student_hbm, student))

    def own_copy(which, k, target):
        return pltpu.make_async_remote_copy(
            src_ref=sources[which][0],
            dst_ref=sources[which][1].at[me],
            send_sem=send_sem.at[which, k],
            recv_sem=recv_sem.at[which, k],
            device_id=spot(target),
            device_id_type=MESH,
        )

    def pass_copy(which, k, source):
        buffer = sources[which][1]
        return pltpu.make_async_remote_copy(
            src_ref=buffer.at[source],
            dst_ref=buffer.at[source],
            send_sem=pass_send.at[which, k],
            recv_sem=pass_recv.at[which, k],
            device_id=spot(sibling),
            device_id_type=MESH,
        )

    pl.semaphore_wait(barrier, n - 1)

    def send_own(k, carry):
        for which in range(2):
            own_copy(which, k + 1, shifted(k + 1, 1) * 2 + core).start()
        return carry

    repeat(chips - 1, send_own)
    for which in range(2):
        own_copy(which, 0, sibling).start()

    for load in loads:
        load.wait()
    lane = lax.broadcasted_iota(jnp.int32, (rows, LANES), 1)
    for pair in range(pairs):
        for inner in range(group):
            at = pl.ds((pair * group + inner) * rows, rows)
            keep = lane // HEAD_DIM == inner
            columns = pl.ds(pair * LANES, LANES)
            own_teacher[at, :] = jnp.where(keep, teacher[me, :, columns], jnp.zeros((), jnp.bfloat16))
            own_student[at, :] = jnp.where(keep, student[me, :, columns], jnp.zeros((), jnp.bfloat16))

    def score(block, first):
        bias = jnp.where(table[me, block] >= 0, 0.0, floor_value).astype(jnp.float32)
        for own, whole, scores, top in (
            (own_teacher, teacher, t_scores, t_top),
            (own_student, student, s_scores, s_top),
        ):
            for pair in range(pairs):
                at = pl.ds(pair * group * rows, group * rows)
                raw = lax.dot_general(
                    own[at, :],
                    whole[block, :, pl.ds(pair * LANES, LANES)],
                    (((1,), (1,)), ((), ())),
                    preferred_element_type=jnp.float32,
                )
                tile = raw * score_factor + bias
                scores[block, at, :] = tile
                top[at, :] = tile if first else jnp.maximum(top[at, :], tile)

    score(me, True)
    for which in range(2):
        own_copy(which, 0, sibling).wait_recv()
    score(sibling, False)

    def direct_turn(k, carry):
        source = shifted(k + 1, -1) * 2 + core
        for which in range(2):
            own_copy(which, k + 1, source).wait_recv()
            pass_copy(which, k + 1, source).start()
        score(source, False)
        return carry

    repeat(chips - 1, direct_turn)

    def passed_turn(k, carry):
        source = shifted(k + 1, -1) * 2 + 1 - core
        for which in range(2):
            pass_copy(which, k + 1, source).wait_recv()
        score(source, False)
        return carry

    repeat(chips - 1, passed_turn)

    wide = jnp.zeros((rows, LANES), jnp.float32)
    for head in range(heads):
        at = pl.ds(head * rows, rows)
        t_high = jnp.max(t_top[at, :], axis=1, keepdims=True)
        s_high = jnp.max(s_top[at, :], axis=1, keepdims=True)
        blank = jnp.zeros((rows, LANES), jnp.float32)

        def sum_turn(block, carry):
            t_sum, s_sum, gap_sum = carry
            t_tile, s_tile = t_scores[block, at, :], s_scores[block, at, :]
            t_exp = jnp.exp2(t_tile - t_high)
            return (
                t_sum + t_exp,
                s_sum + jnp.exp2(s_tile - s_high),
                gap_sum + t_exp * (t_tile - s_tile),
            )

        t_sum, s_sum, gap_sum = [
            jnp.sum(part, axis=1, keepdims=True)
            for part in repeat(n, sum_turn, (blank, blank, blank))
        ]
        t_line = t_high + jnp.log2(t_sum)
        s_line = s_high + jnp.log2(s_sum)
        div_line = gap_sum / t_sum - t_line + s_line
        t_log[at, :] = jnp.broadcast_to(t_line, (rows, LANES))
        s_log[at, :] = jnp.broadcast_to(s_line, (rows, LANES))
        wide = jnp.where(lane == head, t_line, wide)
        wide = jnp.where(lane == heads + head, s_line, wide)
        wide = jnp.where(lane == 2 * heads + head, div_line, wide)
    stats[me] = wide.T[: stats.shape[1]]

    def stat_copy(d, target):
        return pltpu.make_async_remote_copy(
            src_ref=stats.at[me],
            dst_ref=stats.at[me],
            send_sem=stat_send.at[d],
            recv_sem=stat_recv.at[d],
            device_id=spot(target),
            device_id_type=MESH,
        )

    def send_stats(d, carry):
        stat_copy(d + 1, (me + d + 1) % n).start()
        return carry

    repeat(n - 1, send_stats)

    def row_turn(block, carry):
        for head in range(heads):
            at = pl.ds(head * rows, rows)
            row_part[block, at, :] = jnp.exp2(s_scores[block, at, :] - s_log[at, :]) - jnp.exp2(
                t_scores[block, at, :] - t_log[at, :]
            )
        return carry

    repeat(n, row_turn)

    def gradient(block, first):
        for pair in range(pairs):
            parts = []
            for inner in range(group):
                head = pair * group + inner
                at = pl.ds(head * rows, rows)
                t_line = stats[block, pl.ds(head, 1), :]
                s_line = stats[block, pl.ds(heads + head, 1), :]
                column_part = jnp.exp2(s_scores[block, at, :] - s_line) - jnp.exp2(
                    t_scores[block, at, :] - t_line
                )
                parts.append((row_part[block, at, :] + column_part).astype(jnp.bfloat16))
            at = pl.ds(pair * group * rows, group * rows)
            piece = jnp.dot(
                jnp.concatenate(parts, axis=0),
                student[block, :, pl.ds(pair * LANES, LANES)],
                preferred_element_type=jnp.float32,
            )
            total[at, :] = piece if first else total[at, :] + piece

    gradient(me, True)

    def gradient_turn(d, carry):
        source = (me - d - 1 + n) % n
        stat_copy(d + 1, source).wait_recv()
        gradient(source, False)
        return carry

    repeat(n - 1, gradient_turn)

    for pair in range(pairs):
        chosen = total[pl.ds(pair * group * rows, rows), :]
        for inner in range(1, group):
            chosen = jnp.where(
                lane // HEAD_DIM == inner,
                total[pl.ds((pair * group + inner) * rows, rows), :],
                chosen,
            )
        grad_ref[:, pl.ds(pair * LANES, LANES)] = (
            chosen * (distill_weight * HEAD_DIM ** (-0.5))
        ).astype(jnp.bfloat16)

    def div_turn(block, carry):
        return carry + stats[block]

    div_sum = repeat(n, div_turn, jnp.zeros(stats.shape[1:], jnp.float32))
    div_sum = jnp.sum(div_sum, axis=1, keepdims=True) * (math.log(2.0) / (rows * n))
    row_at = lax.broadcasted_iota(jnp.int32, stats.shape[1:], 0)
    lane_at = lax.broadcasted_iota(jnp.int32, stats.shape[1:], 1)
    div_row = jnp.sum(
        jnp.where(row_at == 2 * heads + lane_at, div_sum, 0.0), axis=0, keepdims=True
    )
    div_ref[...] = div_row[:, :heads]

    for which in range(2):
        own_copy(which, 0, sibling).wait_send()

    def drain(k, carry):
        for which in range(2):
            own_copy(which, k + 1, sibling).wait_send()
            pass_copy(which, k + 1, me).wait_send()
        return carry

    repeat(chips - 1, drain)

    def drain_stats(d, carry):
        stat_copy(d + 1, sibling).wait_send()
        return carry

    repeat(n - 1, drain_stats)


def per_device(n, teacher_q, student_q, owner_table):
    rows, width = teacher_q.shape
    heads = width // HEAD_DIM
    chips = n // 2
    stat_rows = -(-3 * heads // 8) * 8
    hbm = pl.BlockSpec(memory_space=pl.ANY)
    grad, divergence = pl.pallas_call(
        functools.partial(kernel, n),
        out_shape=(
            jax.ShapeDtypeStruct((rows, width), jnp.bfloat16),
            jax.ShapeDtypeStruct((1, heads), jnp.float32),
        ),
        in_specs=[hbm, hbm, pl.BlockSpec(memory_space=pltpu.SMEM)],
        out_specs=(
            pl.BlockSpec(memory_space=pltpu.VMEM),
            pl.BlockSpec(memory_space=pltpu.VMEM),
        ),
        scratch_shapes=[
            pltpu.VMEM((n, rows, width), jnp.bfloat16),
            pltpu.VMEM((n, rows, width), jnp.bfloat16),
            pltpu.VMEM((heads * rows, LANES), jnp.bfloat16),
            pltpu.VMEM((heads * rows, LANES), jnp.bfloat16),
            pltpu.VMEM((n, heads * rows, rows), jnp.float32),
            pltpu.VMEM((n, heads * rows, rows), jnp.float32),
            pltpu.VMEM((heads * rows, rows), jnp.float32),
            pltpu.VMEM((heads * rows, rows), jnp.float32),
            pltpu.VMEM((heads * rows, LANES), jnp.float32),
            pltpu.VMEM((heads * rows, LANES), jnp.float32),
            pltpu.VMEM((n, heads * rows, rows), jnp.float32),
            pltpu.VMEM((n, stat_rows, rows), jnp.float32),
            pltpu.VMEM((heads * rows, LANES), jnp.float32),
            pltpu.SemaphoreType.DMA((2,)),
            pltpu.SemaphoreType.DMA((2, chips)),
            pltpu.SemaphoreType.DMA((2, chips)),
            pltpu.SemaphoreType.DMA((2, chips)),
            pltpu.SemaphoreType.DMA((2, chips)),
            pltpu.SemaphoreType.DMA((n,)),
            pltpu.SemaphoreType.DMA((n,)),
        ],
        compiler_params=pltpu.CompilerParams(
            collective_id=0, has_side_effects=True, vmem_limit_bytes=60 * 1024 * 1024
        ),
        name="distill",
    )(teacher_q, student_q, owner_table)
    return (grad, divergence.reshape(heads))


def solution(mesh):
    placed = (P("tok", "head"), P("tok", "head"), P())
    return jax.shard_map(
        functools.partial(per_device, mesh.shape["tok"]),
        mesh=mesh,
        in_specs=placed,
        out_specs=(P("tok", "head"), P("head")),
        check_vma=False,
    )
```

time: 79.5 us -> 22.6 us (0.28)
  blocking collectives: 59.2 us -> 0 us
  Pallas kernels: 0 us -> 19.7 us
  loops' own time: 6.89 us -> 0 us
  other arithmetic: 4.62 us -> 0 us
  matrix products: 2.91 us -> 0 us
  local copies, waits for them, and re-layouts: 4.75 us -> 1.99 us
    all_gather x4 -> x0, blocking collectives: 42.6 us -> none  [the longest x1 11.7 us: per_device(): lax.all_gather(own_logsum[0], 'tok', axis=1, tiled=True)]
    pallas_call x0 -> x1, Pallas kernels: none -> 19.7 us  [per_device(): pl.pallas_call(functools.partial(kernel, n), out_shape=(jax.ShapeDtypeStr...]
    psum x1 -> x0, blocking collectives: 16.5 us -> none  [per_device(): divergence = lax.psum(divergence, 'tok') / (block_rows * block_count)]
    another operation x2 -> x0, loops' own time: 6.89 us -> none  [the longest x1 3.45 us: per_device(): lax.fori_loop(0, column_total, gradient_turn, (start_grad, jnp.zeros((hea...]
    dot_general x10 -> x0, matrix products: 2.91 us -> none  [the longest x8 2.19 us: tile_scores(): jnp.einsum('ahd,bhd->hab', left_block, right_block, preferred_element_typ...]
    dynamic_slice x12 -> x0, local copies, waits for them, and re-layouts: 2.88 us -> none  [the longest x2 1.33 us: row_turn(): column = columns[slot_index]]
    reduce_sum x6 -> x0, other arithmetic: 1.69 us -> none  [the longest x1 1.33 us: per_device(): column_total = jnp.sum(inside_row.astype(jnp.int32))]
    unnamed x5 -> x4, local copies, waits for them, and re-layouts: 1.84 us -> 1.99 us
where the time goes in v1:
time: 22.6 us; the launch traced here: 22.4 us
  Pallas kernels  19.7 us (87%)
  local copies, waits for them, and re-layouts  1.99 us (9%)
  between operations  0.65 us (3%)
    pallas_call x1, Pallas kernels, per_device(): pl.pallas_call(functools.partial(kernel, n), out_shape=(jax.ShapeDtypeStr...  19.7 us
    unnamed x4, local copies, waits for them, and re-layouts  1.99 us

profile of v1, /device:TPU:0, one launch (start us, length us, event | category | flops | bytes accessed | tf_op | source)
XLA Modules:
  0.0 22.4 jit_solution(17301130525647713749)
XLA Ops:
  0.6 19.7 %distill.1 = (bf16[128,256]{1,0:T(8,128)(2,1)}, f32[1,4]{1,0:T(1,128)}) custom-call(bf16[128,256]{1,0:T(8,128)(2,1)} %teacher_hbm.1, bf16[128,256]{1,0:T(8,128)(2,1)} %student_hbm.1, s32[8,8]{1,0:T(8,128)} %table.1), custom_call_target="tpu_custom_call" | custom-call | tf_op jit(solution)/shard_map/distill/pallas_call | solution.py:289
  20.4 0.0 copy-start
  20.4 1.5 %copy.7 = bf16[128,256]{1,0:T(8,128)(2,1)} copy(bf16[128,256]{1,0:T(8,128)(2,1)} %get-tuple-element.8) | data formatting | bytes 131072
  21.9 0.0 copy-done
  21.9 0.5 %copy.8 = f32[4]{0:T(128)} copy(f32[4]{0:T(128)S(1)} %bitcast.1) | data formatting | bytes 32
Async XLA Ops:
  20.4 1.5 %copy-start = (f32[1,4]{1,0:T(1,128)S(1)}, f32[1,4]{1,0:T(1,128)}, u32[]{:S(2)}) copy-start(f32[1,4]{1,0:T(1,128)} %get-tuple-element.5) | copy-start | bytes 52

commit v2 on v1

v2 whole, which is shorter than its diff:
```python
import functools
import math

import jax
import jax.numpy as jnp
from jax import lax
from jax.experimental import pallas as pl
from jax.experimental.pallas import tpu as pltpu
from jax.sharding import PartitionSpec as P

HEAD_DIM = 64
LANES = 128
floor_value = -1e30
distill_weight = 32.0
score_factor = HEAD_DIM ** (-0.5) * math.log2(math.e)
MESH = pl.DeviceIdType.MESH


def repeat(count, body, init=None):
    if count <= 8:
        for step in range(count):
            init = body(step, init)
        return init
    return lax.fori_loop(0, count, body, init)


def kernel(
    n, teacher_hbm, student_hbm, table, grad_ref, div_ref,
    teacher, student, outbox, inbox, own, scores, top, logs, row_part, stats, total,
    out_grad, in_grad, out_div, in_div,
    local_sem, send_sem, recv_sem, stat_send, stat_recv, back_send, back_recv,
):
    rows, width = teacher_hbm.shape
    pairs = width // LANES
    heads = width // HEAD_DIM
    group = LANES // HEAD_DIM
    parts = n // heads
    chips = n // 2
    side = math.isqrt(chips)
    side = side if side * side == chips else 1
    span = chips // side
    half = rows // 2
    own_rows = heads * rows
    me = lax.axis_index("tok")
    head_at = lax.axis_index("head")
    chip, core = me // 2, me % 2
    head, part = me // parts, me % parts

    def spot(tok):
        return (head_at, tok)

    def shifted(k, sign):
        high = (chip // span + sign * (k // span) + side) % side
        low = (chip % span + sign * (k % span) + span) % span
        return high * span + low

    def remote(src, dst, send, recv, target):
        return pltpu.make_async_remote_copy(
            src_ref=src, dst_ref=dst, send_sem=send, recv_sem=recv,
            device_id=spot(target), device_id_type=MESH,
        )

    barrier = pltpu.get_barrier_semaphore()
    loads = [
        pltpu.make_async_copy(teacher_hbm, teacher, local_sem.at[0]),
        pltpu.make_async_copy(student_hbm, student, local_sem.at[1]),
    ]
    for load in loads:
        load.start()

    def greet(d, carry):
        pl.semaphore_signal(barrier, inc=1, device_id=spot((me + d + 1) % n), device_id_type=MESH)
        return carry

    repeat(n - 1, greet)
    for load in loads:
        load.wait()
    lane = lax.broadcasted_iota(jnp.int32, (rows, LANES), 1)
    lower = lane < HEAD_DIM
    for pair in range(pairs):
        columns = pl.ds(pair * LANES, LANES)
        t_pair = teacher[:, columns].astype(jnp.float32)
        s_pair = student[:, columns].astype(jnp.float32)
        outbox[pair * group] = jnp.where(lower, t_pair, pltpu.roll(s_pair, HEAD_DIM, 1)).astype(
            jnp.bfloat16
        )
        outbox[pair * group + 1] = jnp.where(
            lower, pltpu.roll(t_pair, HEAD_DIM, 1), s_pair
        ).astype(jnp.bfloat16)
    inbox[pl.ds(me * rows, rows), :] = outbox[head]
    pl.semaphore_wait(barrier, n - 1)

    def query_copy(k, other, target):
        return remote(
            outbox.at[target // parts],
            inbox.at[pl.ds(me * rows, rows), :],
            send_sem.at[k, other],
            recv_sem.at[k, other],
            target,
        )

    def away(k, other, sign):
        return shifted(k, sign) * 2 + (1 - core if other else core)

    def send_queries(step, carry):
        k = chips - 1 - step
        for other in range(2):
            query_copy(k, other, away(k, other, 1)).start()
        return carry

    repeat(chips - 1, send_queries)
    query_copy(0, 1, away(0, 1, 1)).start()

    query_copy(0, 1, away(0, 1, -1)).wait_recv()

    def take_queries(step, carry):
        for other in range(2):
            query_copy(step + 1, other, away(step + 1, other, -1)).wait_recv()
        return carry

    repeat(chips - 1, take_queries)

    none = jnp.zeros((), jnp.bfloat16)
    for place in range(heads):
        block = inbox[pl.ds((part * heads + place) * rows, rows), :]
        own[pl.ds(place * rows, rows), :] = jnp.where(lower, block, none)
        own[pl.ds(own_rows + place * rows, rows), :] = jnp.where(lower, none, block)

    top[...] = jnp.full(top.shape, 2 * floor_value, jnp.float32)

    def score_turn(step, carry):
        right = inbox[pl.ds(step * 2 * rows, 2 * rows), :]
        raw = lax.dot_general(
            own[...], right, (((1,), (1,)), ((), ())), preferred_element_type=jnp.float32
        )
        for place in range(heads):
            for near in range(2):
                block = step * 2 + near
                bias = jnp.where(table[part * heads + place, block] >= 0, 0.0, floor_value)
                for which in range(2):
                    begin = which * own_rows + place * rows
                    at = pl.ds(begin, rows)
                    tile = (
                        raw[begin : begin + rows, near * rows : (near + 1) * rows] * score_factor
                        + bias.astype(jnp.float32)
                    )
                    scores[block, at, :] = tile
                    top[at, :] = jnp.maximum(top[at, :], tile)
        return carry

    repeat(n // 2, score_turn)

    wide = jnp.zeros((rows, LANES), jnp.float32)
    for place in range(heads):
        t_at, s_at = pl.ds(place * rows, rows), pl.ds(own_rows + place * rows, rows)
        t_high = jnp.max(top[t_at, :], axis=1, keepdims=True)
        s_high = jnp.max(top[s_at, :], axis=1, keepdims=True)
        blank = jnp.zeros((rows, LANES), jnp.float32)

        def sum_turn(block, carry):
            t_sum, s_sum, gap_sum = carry
            t_tile, s_tile = scores[block, t_at, :], scores[block, s_at, :]
            t_exp = jnp.exp2(t_tile - t_high)
            return (
                t_sum + t_exp,
                s_sum + jnp.exp2(s_tile - s_high),
                gap_sum + t_exp * (t_tile - s_tile),
            )

        t_sum, s_sum, gap_sum = [
            jnp.sum(piece, axis=1, keepdims=True)
            for piece in repeat(n, sum_turn, (blank, blank, blank))
        ]
        t_line = t_high + jnp.log2(t_sum)
        s_line = s_high + jnp.log2(s_sum)
        div_line = gap_sum / t_sum - t_line + s_line
        logs[t_at, :] = jnp.broadcast_to(t_line, (rows, LANES))
        logs[s_at, :] = jnp.broadcast_to(s_line, (rows, LANES))
        wide = jnp.where(lane == place, t_line, wide)
        wide = jnp.where(lane == heads + place, s_line, wide)
        wide = jnp.where(lane == 2 * heads + place, div_line, wide)
    stats[part] = wide.T[: stats.shape[1]]

    def stat_copy(step, target):
        return remote(
            stats.at[part], stats.at[part], stat_send.at[step], stat_recv.at[step], target
        )

    def send_stats(step, carry):
        stat_copy(step, head * parts + (part + step + 1) % parts).start()
        return carry

    repeat(parts - 1, send_stats)

    def row_turn(block, carry):
        for place in range(heads):
            t_at, s_at = pl.ds(place * rows, rows), pl.ds(own_rows + place * rows, rows)
            row_part[block, t_at, :] = jnp.exp2(scores[block, s_at, :] - logs[s_at, :]) - jnp.exp2(
                scores[block, t_at, :] - logs[t_at, :]
            )
        return carry

    repeat(n, row_turn)

    def take_stats(step, carry):
        stat_copy(step, head * parts + (part - step - 1 + parts) % parts).wait_recv()
        return carry

    repeat(parts - 1, take_stats)

    def div_turn(step, carry):
        return carry + stats[step, pl.ds(2 * heads, heads), :]

    div_sum = repeat(parts, div_turn, jnp.zeros((heads, rows), jnp.float32))
    div_sum = jnp.sum(jnp.sum(div_sum, axis=0, keepdims=True), axis=1, keepdims=True)
    out_div[...] = jnp.broadcast_to(div_sum * (math.log(2.0) / (rows * n)), out_div.shape)

    def div_copy(place, slot, target):
        return remote(out_div, in_div.at[head], back_send.at[1, place], back_recv.at[1, slot], target)

    def grad_copy(place, slot, target):
        return remote(
            out_grad.at[place], in_grad.at[head], back_send.at[0, place], back_recv.at[0, slot], target
        )

    for place in range(heads):
        target = part * heads + place

        @pl.when(target != me)
        def send_div():
            div_copy(place, head, target).start()

        @pl.when(target == me)
        def keep_div():
            in_div[head] = out_div[...]

    def gradient_turn(step, carry):
        lines = []
        for place in range(heads):
            t_at, s_at = pl.ds(place * rows, rows), pl.ds(own_rows + place * rows, rows)
            pieces = []
            for near in range(2):
                block = step * 2 + near
                line = stats.at[block // heads]
                t_line = line[pl.ds(block % heads, 1), :]
                s_line = line[pl.ds(heads + block % heads, 1), :]
                column_part = jnp.exp2(scores[block, s_at, :] - s_line) - jnp.exp2(
                    scores[block, t_at, :] - t_line
                )
                pieces.append((row_part[block, t_at, :] + column_part).astype(jnp.bfloat16))
            lines.append(jnp.concatenate(pieces, axis=1))
        piece = jnp.dot(
            jnp.concatenate(lines, axis=0),
            inbox[pl.ds(step * 2 * rows, 2 * rows), :],
            preferred_element_type=jnp.float32,
        )
        total[...] = piece if isinstance(step, int) and step == 0 else total[...] + piece
        return carry

    if n // 2 > 8:
        total[...] = jnp.zeros(total.shape, jnp.float32)
    repeat(n // 2, gradient_turn)

    half_lower = lax.broadcasted_iota(jnp.int32, (half, LANES), 1) < HEAD_DIM
    for place in range(heads):
        target = part * heads + place
        upper_rows = total[pl.ds(place * rows, half), :]
        lower_rows = total[pl.ds(place * rows + half, half), :]
        out_grad[place] = (
            jnp.where(half_lower, pltpu.roll(upper_rows, HEAD_DIM, 1), lower_rows)
            * (distill_weight * HEAD_DIM ** (-0.5))
        ).astype(jnp.bfloat16)

        @pl.when(target != me)
        def send_grad():
            grad_copy(place, head, target).start()

        @pl.when(target == me)
        def keep_grad():
            in_grad[head] = out_grad[place]

    for slot in range(heads):
        source = slot * parts + me // heads

        @pl.when(source != me)
        def take_back():
            div_copy(0, slot, source).wait_recv()
            grad_copy(0, slot, source).wait_recv()

    for pair in range(pairs):
        first = in_grad[pair * group].astype(jnp.float32)
        second = in_grad[pair * group + 1].astype(jnp.float32)
        columns = pl.ds(pair * LANES, LANES)
        grad_ref[pl.ds(0, half), columns] = jnp.where(
            half_lower, first, pltpu.roll(second, HEAD_DIM, 1)
        ).astype(jnp.bfloat16)
        grad_ref[pl.ds(half, half), columns] = jnp.where(
            half_lower, pltpu.roll(first, HEAD_DIM, 1), second
        ).astype(jnp.bfloat16)
    div_lane = lax.broadcasted_iota(jnp.int32, (1, LANES), 1)
    div_row = jnp.zeros((1, LANES), jnp.float32)
    for slot in range(heads):
        div_row = jnp.where(div_lane == slot, in_div[slot, pl.ds(0, 1), :], div_row)
    div_ref[...] = div_row[:, :heads]

    query_copy(0, 1, away(0, 1, 1)).wait_send()

    def drain(step, carry):
        for other in range(2):
            query_copy(step + 1, other, away(step + 1, other, 1)).wait_send()
        return carry

    repeat(chips - 1, drain)

    def drain_stats(step, carry):
        stat_copy(step, head * parts + (part + step + 1) % parts).wait_send()
        return carry

    repeat(parts - 1, drain_stats)
    for place in range(heads):
        target = part * heads + place

        @pl.when(target != me)
        def drain_back():
            div_copy(place, head, target).wait_send()
            grad_copy(place, head, target).wait_send()


def per_device(n, teacher_q, student_q, owner_table):
    rows, width = teacher_q.shape
    heads = width // HEAD_DIM
    chips = n // 2
    parts = n // heads
    stat_rows = -(-3 * heads // 8) * 8
    hbm = pl.BlockSpec(memory_space=pl.ANY)
    grad, divergence = pl.pallas_call(
        functools.partial(kernel, n),
        out_shape=(
            jax.ShapeDtypeStruct((rows, width), jnp.bfloat16),
            jax.ShapeDtypeStruct((1, heads), jnp.float32),
        ),
        in_specs=[hbm, hbm, pl.BlockSpec(memory_space=pltpu.SMEM)],
        out_specs=(
            pl.BlockSpec(memory_space=pltpu.VMEM),
            pl.BlockSpec(memory_space=pltpu.VMEM),
        ),
        scratch_shapes=[
            pltpu.VMEM((rows, width), jnp.bfloat16),
            pltpu.VMEM((rows, width), jnp.bfloat16),
            pltpu.VMEM((heads, rows, LANES), jnp.bfloat16),
            pltpu.VMEM((n * rows, LANES), jnp.bfloat16),
            pltpu.VMEM((2 * heads * rows, LANES), jnp.bfloat16),
            pltpu.VMEM((n, 2 * heads * rows, rows), jnp.float32),
            pltpu.VMEM((2 * heads * rows, rows), jnp.float32),
            pltpu.VMEM((2 * heads * rows, LANES), jnp.float32),
            pltpu.VMEM((n, heads * rows, rows), jnp.float32),
            pltpu.VMEM((parts, stat_rows, rows), jnp.float32),
            pltpu.VMEM((heads * rows, LANES), jnp.float32),
            pltpu.VMEM((heads, rows // 2, LANES), jnp.bfloat16),
            pltpu.VMEM((heads, rows // 2, LANES), jnp.bfloat16),
            pltpu.VMEM((8, LANES), jnp.float32),
            pltpu.VMEM((heads, 8, LANES), jnp.float32),
            pltpu.SemaphoreType.DMA((2,)),
            pltpu.SemaphoreType.DMA((chips, 2)),
            pltpu.SemaphoreType.DMA((chips, 2)),
            pltpu.SemaphoreType.DMA((parts,)),
            pltpu.SemaphoreType.DMA((parts,)),
            pltpu.SemaphoreType.DMA((2, heads)),
            pltpu.SemaphoreType.DMA((2, heads)),
        ],
        compiler_params=pltpu.CompilerParams(
            collective_id=0, has_side_effects=True, vmem_limit_bytes=60 * 1024 * 1024
        ),
        name="distill",
    )(teacher_q, student_q, owner_table)
    return (grad, divergence.reshape(heads))


def solution(mesh):
    placed = (P("tok", "head"), P("tok", "head"), P())
    return jax.shard_map(
        functools.partial(per_device, mesh.shape["tok"]),
        mesh=mesh,
        in_specs=placed,
        out_specs=(P("tok", "head"), P("head")),
        check_vma=False,
    )
```

time: 22.6 us -> 19.6 us (0.87)
  Pallas kernels: 19.7 us -> 16.7 us
    pallas_call x1, Pallas kernels: 19.7 us -> 16.7 us  [per_device(): pl.pallas_call(functools.partial(kernel, n), out_shape=(jax.ShapeDtypeStr...]
where the time goes in v2:
time: 19.6 us; the launch traced here: 19.3 us
  Pallas kernels  16.7 us (85%)
  local copies, waits for them, and re-layouts  1.99 us (10%)
  between operations  0.65 us (3%)
    pallas_call x1, Pallas kernels, per_device(): pl.pallas_call(functools.partial(kernel, n), out_shape=(jax.ShapeDtypeStr...  16.7 us
    unnamed x4, local copies, waits for them, and re-layouts  1.99 us

profile of v2, /device:TPU:0, one launch (start us, length us, event | category | flops | bytes accessed | tf_op | source)
XLA Modules:
  0.0 19.3 jit_solution(14662387752548261972)
XLA Ops:
  0.6 16.7 %distill.1 = (bf16[128,256]{1,0:T(8,128)(2,1)}, f32[1,4]{1,0:T(1,128)}) custom-call(bf16[128,256]{1,0:T(8,128)(2,1)} %teacher_hbm.1, bf16[128,256]{1,0:T(8,128)(2,1)} %student_hbm.1, s32[8,8]{1,0:T(8,128)} %table.1), custom_call_target="tpu_custom_call" | custom-call | tf_op jit(solution)/shard_map/distill/pallas_call | solution.py:336
  17.3 0.0 copy-start
  17.3 1.5 %copy.7 = bf16[128,256]{1,0:T(8,128)(2,1)} copy(bf16[128,256]{1,0:T(8,128)(2,1)} %get-tuple-element.8) | data formatting | bytes 131072
  18.8 0.0 copy-done
  18.8 0.5 %copy.8 = f32[4]{0:T(128)} copy(f32[4]{0:T(128)S(1)} %bitcast.1) | data formatting | bytes 32
Async XLA Ops:
  17.3 1.5 %copy-start = (f32[1,4]{1,0:T(1,128)S(1)}, f32[1,4]{1,0:T(1,128)}, u32[]{:S(2)}) copy-start(f32[1,4]{1,0:T(1,128)} %get-tuple-element.5) | copy-start | bytes 52

commit v3 on v2

--- a/solution.py
+++ b/solution.py
@@ -25,10 +25,9 @@
 
 
 def kernel(
-    n, teacher_hbm, student_hbm, table, grad_ref, div_ref,
-    teacher, student, outbox, inbox, own, scores, top, logs, row_part, stats, total,
-    out_grad, in_grad, out_div, in_div,
-    local_sem, send_sem, recv_sem, stat_send, stat_recv, back_send, back_recv,
+    n, teacher_hbm, student_hbm, table, in_grad, in_div,
+    teacher, student, outbox, inbox, own, scores, top, logs, row_part, stats,
+    out_grad, out_div, local_sem, send_sem, recv_sem, stat_send, stat_recv, back_send, back_recv,
 ):
     rows, width = teacher_hbm.shape
     pairs = width // LANES
@@ -232,52 +231,58 @@
 
         @pl.when(target == me)
         def keep_div():
-            in_div[head] = out_div[...]
-
-    def gradient_turn(step, carry):
-        lines = []
-        for place in range(heads):
-            t_at, s_at = pl.ds(place * rows, rows), pl.ds(own_rows + place * rows, rows)
-            pieces = []
-            for near in range(2):
-                block = step * 2 + near
-                line = stats.at[block // heads]
-                t_line = line[pl.ds(block % heads, 1), :]
-                s_line = line[pl.ds(heads + block % heads, 1), :]
-                column_part = jnp.exp2(scores[block, s_at, :] - s_line) - jnp.exp2(
-                    scores[block, t_at, :] - t_line
-                )
-                pieces.append((row_part[block, t_at, :] + column_part).astype(jnp.bfloat16))
-            lines.append(jnp.concatenate(pieces, axis=1))
-        piece = jnp.dot(
-            jnp.concatenate(lines, axis=0),
-            inbox[pl.ds(step * 2 * rows, 2 * rows), :],
-            preferred_element_type=jnp.float32,
-        )
-        total[...] = piece if isinstance(step, int) and step == 0 else total[...] + piece
-        return carry
-
-    if n // 2 > 8:
-        total[...] = jnp.zeros(total.shape, jnp.float32)
-    repeat(n // 2, gradient_turn)
+            keep = pltpu.make_async_copy(out_div, in_div.at[head], local_sem.at[0])
+            keep.start()
+            keep.wait()
 
     half_lower = lax.broadcasted_iota(jnp.int32, (half, LANES), 1) < HEAD_DIM
-    for place in range(heads):
-        target = part * heads + place
-        upper_rows = total[pl.ds(place * rows, half), :]
-        lower_rows = total[pl.ds(place * rows + half, half), :]
-        out_grad[place] = (
-            jnp.where(half_lower, pltpu.roll(upper_rows, HEAD_DIM, 1), lower_rows)
-            * (distill_weight * HEAD_DIM ** (-0.5))
-        ).astype(jnp.bfloat16)
-
-        @pl.when(target != me)
-        def send_grad():
-            grad_copy(place, head, target).start()
-
-        @pl.when(target == me)
-        def keep_grad():
-            in_grad[head] = out_grad[place]
+    run = heads // 2
+    for turn in range(2):
+        place_base = (chip + 1 + turn) % 2 * run
+
+        def gradient_turn(step, carry):
+            lines = []
+            for inner in range(run):
+                place = place_base + inner
+                t_at = pl.ds(pl.multiple_of(place * rows, rows), rows)
+                s_at = pl.ds(pl.multiple_of(own_rows + place * rows, rows), rows)
+                pieces = []
+                for near in range(2):
+                    block = step * 2 + near
+                    line = stats.at[block // heads]
+                    t_line = line[pl.ds(block % heads, 1), :]
+                    s_line = line[pl.ds(heads + block % heads, 1), :]
+                    column_part = jnp.exp2(scores[block, s_at, :] - s_line) - jnp.exp2(
+                        scores[block, t_at, :] - t_line
+                    )
+                    pieces.append((row_part[block, t_at, :] + column_part).astype(jnp.bfloat16))
+                lines.append(jnp.concatenate(pieces, axis=1))
+            return carry + jnp.dot(
+                jnp.concatenate(lines, axis=0),
+                inbox[pl.ds(step * 2 * rows, 2 * rows), :],
+                preferred_element_type=jnp.float32,
+            )
+
+        total = repeat(n // 2, gradient_turn, jnp.zeros((run * rows, LANES), jnp.float32))
+        for inner in range(run):
+            place = place_base + inner
+            target = part * heads + place
+            upper_rows = total[inner * rows : inner * rows + half]
+            lower_rows = total[inner * rows + half : (inner + 1) * rows]
+            out_grad[place] = (
+                jnp.where(half_lower, pltpu.roll(upper_rows, HEAD_DIM, 1), lower_rows)
+                * (distill_weight * HEAD_DIM ** (-0.5))
+            ).astype(jnp.bfloat16)
+
+            @pl.when(target != me)
+            def send_grad():
+                grad_copy(place, head, target).start()
+
+    @pl.when(part == me // heads)
+    def keep_grad():
+        keep = pltpu.make_async_copy(out_grad.at[me % heads], in_grad.at[head], local_sem.at[1])
+        keep.start()
+        keep.wait()
 
     for slot in range(heads):
         source = slot * parts + me // heads
@@ -287,7 +292,34 @@
             div_copy(0, slot, source).wait_recv()
             grad_copy(0, slot, source).wait_recv()
 
-    for pair in range(pairs):
+    query_copy(0, 1, away(0, 1, 1)).wait_send()
+
+    def drain(step, carry):
+        for other in range(2):
+            query_copy(step + 1, other, away(step + 1, other, 1)).wait_send()
+        return carry
+
+    repeat(chips - 1, drain)
+
+    def drain_stats(step, carry):
+        stat_copy(step, head * parts + (part + step + 1) % parts).wait_send()
+        return carry
+
+    repeat(parts - 1, drain_stats)
+    for place in range(heads):
+        target = part * heads + place
+
+        @pl.when(target != me)
+        def drain_back():
+            div_copy(place, head, target).wait_send()
+            grad_copy(place, head, target).wait_send()
+
+
+def unpack(in_grad, in_div, grad_ref, div_ref):
+    heads, half = in_grad.shape[:2]
+    group = LANES // HEAD_DIM
+    half_lower = lax.broadcasted_iota(jnp.int32, (half, LANES), 1) < HEAD_DIM
+    for pair in range(heads // group):
         first = in_grad[pair * group].astype(jnp.float32)
         second = in_grad[pair * group + 1].astype(jnp.float32)
         columns = pl.ds(pair * LANES, LANES)
@@ -303,28 +335,6 @@
         div_row = jnp.where(div_lane == slot, in_div[slot, pl.ds(0, 1), :], div_row)
     div_ref[...] = div_row[:, :heads]
 
-    query_copy(0, 1, away(0, 1, 1)).wait_send()
-
-    def drain(step, carry):
-        for other in range(2):
-            query_copy(step + 1, other, away(step + 1, other, 1)).wait_send()
-        return carry
-
-    repeat(chips - 1, drain)
-
-    def drain_stats(step, carry):
-        stat_copy(step, head * parts + (part + step + 1) % parts).wait_send()
-        return carry
-
-    repeat(parts - 1, drain_stats)
-    for place in range(heads):
-        target = part * heads + place
-
-        @pl.when(target != me)
-        def drain_back():
-            div_copy(place, head, target).wait_send()
-            grad_copy(place, head, target).wait_send()
-
 
 def per_device(n, teacher_q, student_q, owner_table):
     rows, width = teacher_q.shape
@@ -333,17 +343,14 @@
     parts = n // heads
     stat_rows = -(-3 * heads // 8) * 8
     hbm = pl.BlockSpec(memory_space=pl.ANY)
-    grad, divergence = pl.pallas_call(
+    packed = pl.pallas_call(
         functools.partial(kernel, n),
         out_shape=(
-            jax.ShapeDtypeStruct((rows, width), jnp.bfloat16),
-            jax.ShapeDtypeStruct((1, heads), jnp.float32),
+            jax.ShapeDtypeStruct((heads, rows // 2, LANES), jnp.bfloat16),
+            jax.ShapeDtypeStruct((heads, 8, LANES), jnp.float32),
         ),
         in_specs=[hbm, hbm, pl.BlockSpec(memory_space=pltpu.SMEM)],
-        out_specs=(
-            pl.BlockSpec(memory_space=pltpu.VMEM),
-            pl.BlockSpec(memory_space=pltpu.VMEM),
-        ),
+        out_specs=(hbm, hbm),
         scratch_shapes=[
             pltpu.VMEM((rows, width), jnp.bfloat16),
             pltpu.VMEM((rows, width), jnp.bfloat16),
@@ -355,11 +362,8 @@
             pltpu.VMEM((2 * heads * rows, LANES), jnp.float32),
             pltpu.VMEM((n, heads * rows, rows), jnp.float32),
             pltpu.VMEM((parts, stat_rows, rows), jnp.float32),
-            pltpu.VMEM((heads * rows, LANES), jnp.float32),
-            pltpu.VMEM((heads, rows // 2, LANES), jnp.bfloat16),
             pltpu.VMEM((heads, rows // 2, LANES), jnp.bfloat16),
             pltpu.VMEM((8, LANES), jnp.float32),
-            pltpu.VMEM((heads, 8, LANES), jnp.float32),
             pltpu.SemaphoreType.DMA((2,)),
             pltpu.SemaphoreType.DMA((chips, 2)),
             pltpu.SemaphoreType.DMA((chips, 2)),
@@ -373,6 +377,16 @@
         ),
         name="distill",
     )(teacher_q, student_q, owner_table)
+    grad, divergence = pl.pallas_call(
+        unpack,
+        out_shape=(
+            jax.ShapeDtypeStruct((rows, width), jnp.bfloat16),
+            jax.ShapeDtypeStruct((1, heads), jnp.float32),
+        ),
+        in_specs=[pl.BlockSpec(memory_space=pltpu.VMEM)] * 2,
+        out_specs=(pl.BlockSpec(memory_space=pltpu.VMEM),) * 2,
+        name="unpack",
+    )(*packed)
     return (grad, divergence.reshape(heads))
 
 

time: 19.6 us -> 18.2 us (0.929)
  local copies, waits for them, and re-layouts: 1.99 us -> 0 us
  Pallas kernels: 16.7 us -> 17.4 us
    unnamed x4 -> x0, local copies, waits for them, and re-layouts: 1.99 us -> none
    pallas_call x0 -> x1, Pallas kernels: none -> 1.56 us  [per_device(): pl.pallas_call(unpack, out_shape=(jax.ShapeDtypeStruct((rows, width), jnp...]
    pallas_call x1, Pallas kernels: 16.7 us -> 15.8 us  [per_device(): pl.pallas_call(functools.partial(kernel, n), out_shape=(jax.ShapeDtypeStr...]
where the time goes in v3:
time: 18.2 us; the launch traced here: 18 us
  Pallas kernels  17.4 us (96%)
  between operations  0.64 us (4%)
    pallas_call x1, Pallas kernels, per_device(): pl.pallas_call(functools.partial(kernel, n), out_shape=(jax.ShapeDtypeStr...  15.8 us
    pallas_call x1, Pallas kernels, per_device(): pl.pallas_call(unpack, out_shape=(jax.ShapeDtypeStruct((rows, width), jnp...  1.56 us

profile of v3, /device:TPU:0, one launch (start us, length us, event | category | flops | bytes accessed | tf_op | source)
XLA Modules:
  0.0 18.0 jit_solution(5301773437347543626)
XLA Ops:
  0.6 15.8 %distill.1 = (bf16[4,64,128]{2,1,0:T(8,128)(2,1)}, f32[4,8,128]{2,1,0:T(8,128)}) custom-call(bf16[128,256]{1,0:T(8,128)(2,1)} %teacher_hbm.1, bf16[128,256]{1,0:T(8,128)(2,1)} %student_hbm.1, s32[8,8]{1,0:T(8,128)} %table.1), custom_call_target="tpu_custom_call" | custom-call | tf_op jit(solution)/shard_map/distill/pallas_call | solution.py:346
  16.4 1.6 %unpack.1 = (bf16[128,256]{1,0:T(8,128)(2,1)}, f32[1,4]{1,0:T(1,128)}) custom-call(bf16[4,64,128]{2,1,0:T(8,128)(2,1)} %get-tuple-element.6.in_grad, f32[4,8,128]{2,1,0:T(8,128)} %get-tuple-element.7.in_div), custom_call_target="tpu_custom_call" | custom-call | tf_op jit(solution)/shard_map/unpack/pallas_call | solution.py:380
